TPU v7x, 32 devices: a whole 2x2x4 slice. The times are simulated.
32 devices in a mesh: px: 8 (over y, x, core), py: 4 (over z).
Axes of the slice: x: 2, y: 2, z: 4, core: 2. Of those that a mesh axis runs over, the one named last changes fastest.
Arguments:
- velocity: float32 [8, 1024, 1024], P(None, 'px', 'py'), may hold values from -6 to 6
- forcing: bfloat16 [8, 1024, 1024], P(None, 'px', 'py'), may hold values from -6 to 6
- cross_x: bfloat16 [8, 1024, 1024], P(None, 'px', 'py'), may hold values from -1.5 to 1.5
- cross_y: bfloat16 [8, 1024, 1024], P(None, 'px', 'py'), may hold values from -1.5 to 1.5
- inv_x: bfloat16 [8, 1024, 1024], P('px'), may hold values from -1 to 2, as said below
- inv_y: bfloat16 [8, 1024, 1024], P('px'), may hold values from -1 to 2, as said below
Outputs:
- velocity_new: float32 [8, 1024, 1024], P(None, 'px', 'py')
Inputs may be any that keep to these rules, and one draw needn't show every extreme that they name: `inv_x`: a dense matrix for each level. `inv_y`: a dense matrix for each level.
All inputs are finite; a program needn't handle non-finite values.
Results may differ from a plain program's by a relative error of at most 0.0052.
Values may be sent and summed in bfloat16 or wider, within the bound.
A program may use at most 64 MiB of HBM per device.

v0:
```python
import jax
import jax.numpy as jnp
from jax import lax
from jax.sharding import PartitionSpec as P

time_step = 0.25


def with_halo(cells, sides, width):
    for axis, dim in sides:
        count = lax.axis_size(axis)
        head = lax.slice_in_dim(cells, 0, width, axis=dim)
        tail = lax.slice_in_dim(cells, cells.shape[dim] - width, cells.shape[dim], axis=dim)
        cells = jnp.concatenate(
            [
                lax.ppermute(tail, axis, [(i, (i + 1) % count) for i in range(count)]),
                cells,
                lax.ppermute(head, axis, [((i + 1) % count, i) for i in range(count)]),
            ],
            axis=dim,
        )
    return cells


def shards(velocity, forcing, cross_x, cross_y, inv_x, inv_y):
    padded = with_halo(velocity, (("px", 1), ("py", 2)), 1)
    x_plus = padded[:, 2:, 1:-1]
    x_minus = padded[:, :-2, 1:-1]
    y_plus = padded[:, 1:-1, 2:]
    y_minus = padded[:, 1:-1, :-2]
    z_padded = jnp.pad(velocity, ((1, 1), (0, 0), (0, 0)))
    laplace = (
        x_plus
        + x_minus
        + y_plus
        + y_minus
        - 4.0 * velocity
        + z_padded[2:]
        + z_padded[:-2]
        - 2.0 * velocity
    )
    slope_x = jnp.pad(0.5 * (x_plus - x_minus), ((1, 1), (0, 0), (0, 0)))
    slope_y = jnp.pad(0.5 * (y_plus - y_minus), ((1, 1), (0, 0), (0, 0)))
    mixed_x = 0.5 * (slope_x[2:] - slope_x[:-2])
    mixed_y = 0.5 * (slope_y[2:] - slope_y[:-2])
    total = (
        laplace
        + cross_x.astype(jnp.float32) * mixed_x
        + cross_y.astype(jnp.float32) * mixed_y
        + forcing.astype(jnp.float32)
    )
    rhs = (time_step * total).astype(jnp.bfloat16)
    section_one = jnp.einsum(
        "lab,lbk->lak",
        inv_x,
        lax.all_to_all(rhs, "px", split_axis=0, concat_axis=1, tiled=True),
        preferred_element_type=jnp.float32,
    ).astype(jnp.bfloat16)
    y_lines = lax.all_to_all(section_one, "py", split_axis=1, concat_axis=2, tiled=True)
    section_two = jnp.einsum("lxb,lab->lxa", y_lines, inv_y, preferred_element_type=jnp.float32)
    settled = lax.all_to_all(
        lax.all_to_all(section_two, "py", split_axis=2, concat_axis=1, tiled=True),
        "px",
        split_axis=1,
        concat_axis=0,
        tiled=True,
    )
    return velocity + settled


def solution(mesh):
    return jax.shard_map(
        shards,
        mesh=mesh,
        in_specs=(
            P(None, "px", "py"),
            P(None, "px", "py"),
            P(None, "px", "py"),
            P(None, "px", "py"),
            P("px", None, None),
            P("px", None, None),
        ),
        out_specs=P(None, "px", "py"),
        check_vma=False,
    )
```

profile of v0, /device:TPU:0, one launch (start us, length us, event | category | flops | bytes accessed | tf_op | source)
XLA Modules:
  0.0 129.5 jit_solution(139987141800163913)
XLA Ops:
  0.0 0.0 copy-start
  0.0 1.0 fusion.27
  1.1 3.4 %collective-permute-start = (f32[8,1,256]{2,0,1:T(8,128)S(1)}, f32[8,1,256]{2,0,1:T(8,128)S(1)}, u32[]{:S(2)}, u32[]{:S(2)}) collective-permute-start(f32[8,1,256]{2,0,1:T(8,128)S(1)} %copy.85), channel_id=1, source_target_pairs={{4,0},{8,4},{12,8},{16,12},{20,16},{24,20},{28,24},{0,28},{5,1},{9... | collective-permute-start | bytes 24584 | tf_op jit(solution)/shard_map/ppermute | solution.py:18
  4.5 0.0 collective-permute-start.1
  4.5 1.6 %copy.61 = f32[8,128,256]{1,0,2:T(8,128)S(1)} copy(f32[8,128,256]{2,1,0:T(8,128)} %param.6) | data formatting | bytes 2097152 | tf_op args[0]
  6.1 0.0 collective-permute-done
  6.1 1.3 %copy.62 = f32[8,1,256]{1,0,2:T(8,128)} copy(f32[8,1,256]{2,0,1:T(8,128)S(1)} %collective-permute-done) | data formatting | bytes 16384 | tf_op jit(solution)/shard_map/ppermute | solution.py:18
  7.5 1.0 collective-permute-done.1
  8.4 1.3 %copy.64 = f32[8,1,256]{1,0,2:T(8,128)} copy(f32[8,1,256]{2,0,1:T(8,128)S(1)} %collective-permute-done.1) | data formatting | bytes 16384 | tf_op jit(solution)/shard_map/ppermute | solution.py:16
  9.8 0.8 pad_maximum_fusion.8
  10.6 3.6 %collective-permute-start.2 = (f32[8,130,1]{1,0,2:T(8,128)S(1)}, f32[8,130,1]{1,0,2:T(8,128)S(1)}, u32[]{:S(2)}, u32[]{:S(2)}) collective-permute-start(f32[8,130,1]{1,0,2:T(8,128)S(1)} %get-tuple-element.8), channel_id=1, source_target_pairs={{1,0},{2,1},{3,2},{0,3},{5,4},{6,5},{7,6},{4,7},{9,8},{10,9},{11,1... | collective-permute-start | bytes 12488 | tf_op jit(solution)/shard_map/ppermute | solution.py:18
  14.2 0.0 collective-permute-start.3
  14.2 2.1 %copy.72 = bf16[8,128,256]{1,0,2:T(8,128)(2,1)} copy(bf16[8,128,256]{2,1,0:T(8,128)(2,1)} %param.8) | data formatting | bytes 1048576 | tf_op args[2]
  16.3 2.1 %copy.73 = bf16[8,128,256]{1,0,2:T(8,128)(2,1)} copy(bf16[8,128,256]{2,1,0:T(8,128)(2,1)} %param.9) | data formatting | bytes 1048576 | tf_op args[3]
  18.4 2.1 %copy.74 = bf16[8,128,256]{1,0,2:T(8,128)(2,1)} copy(bf16[8,128,256]{2,1,0:T(8,128)(2,1)} %param.7) | data formatting | bytes 1048576 | tf_op args[1]
  20.6 0.0 copy-start.6
  20.6 0.0 collective-permute-done.2
  20.6 0.0 collective-permute-done.3
  20.6 3.8 %subtract_multiply_fusion = (f32[8,128,256]{1,0,2:T(8,128)S(1)}, f32[8,128,256]{1,0,2:T(8,128)S(1)}) fusion(f32[8,130,1]{1,0,2:T(8,128)S(1)} %collective-permute-done.2, f32[8,1,256]{1,0,2:T(8,128)} %copy.62, f32[8,128,256]{1,0,2:T(8,128)S(1)} %copy.61, f32[8,1,256]{1,0,2:T(8,128)} %copy.64, f32[8,130,1]{1,0,2:T(8,128)S(1)} %collective-permute-done.3), kind=kLoop, calls=%fused_computation.35 | loop fusion | flops 3145728 | bytes 3170432 | tf_op jit(solution)/shard_map/mul | solution.py:43
  24.4 0.0 copy-done.1
  24.4 0.0 copy-done.2
  24.4 0.0 copy-done.4
  24.4 0.0 copy-done.5
  24.4 0.0 copy-done.6
  24.5 2.4 %fusion.20 = bf16[8,128,256]{1,0,2:T(8,128)(2,1)S(1)} fusion(f32[8,128,256]{1,0,2:T(8,128)S(1)} %copy.61, f32[8,128,256]{1,0,2:T(8,128)S(1)} %get-tuple-element.6, f32[8,128,256]{1,0,2:T(8,128)S(1)} %get-tuple-element.5, bf16[8,128,256]{1,0,2:T(8,128)(2,1)S(1)} %copy-done.6, bf16[8,128,256]{1,0,2:T(8,128)(2,1)S(1)} %copy-done.5, ...), kind=kLoop, calls=%fused_computation.20 | loop fusion | flops 8126464 | bytes 5267584 | tf_op jit(solution)/shard_map/convert_element_type | solution.py:52
  26.9 0.1 copy.75
  27.0 12.2 %all_to_all.54 = bf16[8,128,256]{1,2,0:T(8,128)(2,1)S(1)} all-to-all(bf16[8,128,256]{1,2,0:T(8,128)(2,1)S(1)} %copy.75), channel_id=1, replica_groups=mesh['px'=8,'py'=4] {'px'}, dimensions={0} | all-to-all | bytes 1048576 | tf_op jit(solution)/shard_map/all_to_all | solution.py:56
  39.2 0.2 copy.76
  39.4 0.0 copy-done
  39.4 1.6 %fusion.10 = bf16[1,1024,256]{1,2,0:T(8,128)(2,1)} fusion(bf16[1024,256]{1,0:T(8,128)(2,1)S(1)} %bitcast.39, bf16[1,1024,1024]{2,1,0:T(8,128)(2,1)S(1)} %copy-done), kind=kOutput, calls=%fused_computation.12 | convolution fusion | flops 537133056 | bytes 3145728 | tf_op jit(solution)/shard_map/lab,lbk->lak/dot_general | solution.py:53
  40.9 2.4 %copy.77 = bf16[1,1024,256]{2,0,1:T(2,128)(2,1)S(1)} copy(bf16[1,1024,256]{1,2,0:T(8,128)(2,1)} %fusion.10) | data formatting | bytes 1048576 | tf_op jit(solution)/shard_map/convert_element_type | solution.py:58
  43.3 0.6 broadcast.13
  43.9 4.6 %reduce = bf16[1024,256]{1,0:T(8,128)(2,1)} reduce(bf16[1024,1,256]{2,1,0:T(2,128)(2,1)S(1)} %bitcast.34, bf16[]{:T(256)} %broadcast.13), dimensions={1}, to_apply=%bitcast.28.reduce_sub_computation | reduce | bytes 1048578
  48.5 1.2 reshape.27
  49.7 18.9 %all_to_all.55 = bf16[4,2,32768]{2,1,0:T(2,128)(2,1)} all-to-all(bf16[4,2,32768]{2,1,0:T(2,128)(2,1)S(1)} %reshape.27), channel_id=1, replica_groups=mesh['px'=8,'py'=4] {'py'}, dimensions={0} | all-to-all | bytes 1048576 | tf_op jit(solution)/shard_map/all_to_all | solution.py:59
  68.5 2.2 %reshape.28 = bf16[1024,1,256]{2,1,0:T(2,128)(2,1)S(1)} reshape(bf16[4,2,32768]{2,1,0:T(2,128)(2,1)} %all_to_all.55) | data formatting | bytes 1048576
  70.8 0.9 copy.82
  71.6 2.0 %copy.78 = bf16[1,256,4,256]{1,3,2,0:T(8,128)(2,1)} copy(bf16[1,256,4,256]{3,1,2,0:T(8,128)(2,1)} %bitcast.37) | data formatting | bytes 1048576 | tf_op jit(solution)/shard_map/all_to_all | solution.py:59
  73.7 2.5 %fusion.4 = f32[1,256,1024]{2,1,0:T(8,128)S(1)} fusion(bf16[256,1024]{0,1:T(8,128)(2,1)} %bitcast.38, bf16[1,1024,1024]{2,1,0:T(8,128)(2,1)} %param.11), kind=kOutput, calls=%fused_computation.10 | convolution fusion | flops 536870912 | bytes 3670016 | tf_op jit(solution)/shard_map/lxb,lab->lxa/dot_general | solution.py:60
  76.2 1.9 %copy.79 = f32[1,256,1024]{1,0,2:T(1,128)} copy(f32[1,256,1024]{2,1,0:T(8,128)S(1)} %fusion.4) | data formatting | bytes 2097152 | tf_op jit(solution)/shard_map/lxb,lab->lxa/dot_general | solution.py:60
  78.1 28.2 %all_to_all.56 = f32[1,256,1024]{1,0,2:T(1,128)S(1)} all-to-all(f32[1,256,1024]{1,0,2:T(1,128)} %copy.79), channel_id=1, replica_groups=mesh['px'=8,'py'=4] {'py'}, dimensions={2} | all-to-all | bytes 2097152 | tf_op jit(solution)/shard_map/all_to_all | solution.py:62
  106.3 0.1 copy.83
  106.4 1.3 %copy.80 = f32[1,4,256,256]{3,2,1,0:T(8,128)} copy(f32[1,4,256,256]{2,3,1,0:T(8,128)S(1)} %bitcast.35) | data formatting | bytes 2097152 | tf_op jit(solution)/shard_map/all_to_all | solution.py:62
  107.7 2.3 %copy.81 = f32[1,1024,256]{2,0,1:T(1,128)S(1)} copy(f32[1,1024,256]{2,1,0:T(8,128)} %bitcast.36) | data formatting | bytes 2097152 | tf_op jit(solution)/shard_map/all_to_all | solution.py:62
  110.0 0.0 copy-start.3
  110.0 18.2 %all_to_all.57 = f32[1,1024,256]{2,0,1:T(1,128)S(1)} all-to-all(f32[1,1024,256]{2,0,1:T(1,128)S(1)} %copy.81), channel_id=1, replica_groups=mesh['px'=8,'py'=4] {'px'}, dimensions={1} | all-to-all | bytes 2097152 | tf_op jit(solution)/shard_map/all_to_all | solution.py:61
  128.3 0.1 copy.84
  128.3 1.1 add.41
  (7 shorter events, 0.0 us)
Async XLA Ops:
  0.0 39.4 %copy-start = (bf16[1,1024,1024]{2,1,0:T(8,128)(2,1)S(1)}, bf16[1,1024,1024]{2,1,0:T(8,128)(2,1)}, u32[]{:S(2)}) copy-start(bf16[1,1024,1024]{2,1,0:T(8,128)(2,1)} %param.10) | copy-start | bytes 6291460
  1.1 5.1 %collective-permute-start = (f32[8,1,256]{2,0,1:T(8,128)S(1)}, f32[8,1,256]{2,0,1:T(8,128)S(1)}, u32[]{:S(2)}, u32[]{:S(2)}) collective-permute-start(f32[8,1,256]{2,0,1:T(8,128)S(1)} %copy.85), channel_id=1, source_target_pairs={{4,0},{8,4},{12,8},{16,12},{20,16},{24,20},{28,24},{0,28},{5,1},{9... | collective-permute-start | bytes 24584 | tf_op jit(solution)/shard_map/ppermute | solution.py:18
  4.5 4.0 %collective-permute-start.1 = (f32[8,1,256]{2,0,1:T(8,128)S(1)}, f32[8,1,256]{2,0,1:T(8,128)S(1)}, u32[]{:S(2)}, u32[]{:S(2)}) collective-permute-start(f32[8,1,256]{2,0,1:T(8,128)S(1)} %copy.86), channel_id=1, source_target_pairs={{0,4},{4,8},{8,12},{12,16},{16,20},{20,24},{24,28},{28,0},{1,5},{5... | collective-permute-start | bytes 24584 | tf_op jit(solution)/shard_map/ppermute | solution.py:16
  10.6 10.0 %collective-permute-start.2 = (f32[8,130,1]{1,0,2:T(8,128)S(1)}, f32[8,130,1]{1,0,2:T(8,128)S(1)}, u32[]{:S(2)}, u32[]{:S(2)}) collective-permute-start(f32[8,130,1]{1,0,2:T(8,128)S(1)} %get-tuple-element.8), channel_id=1, source_target_pairs={{1,0},{2,1},{3,2},{0,3},{5,4},{6,5},{7,6},{4,7},{9,8},{10,9},{11,1... | collective-permute-start | bytes 12488 | tf_op jit(solution)/shard_map/ppermute | solution.py:18
  14.2 6.4 %collective-permute-start.3 = (f32[8,130,1]{1,0,2:T(8,128)S(1)}, f32[8,130,1]{1,0,2:T(8,128)S(1)}, u32[]{:S(2)}, u32[]{:S(2)}) collective-permute-start(f32[8,130,1]{1,0,2:T(8,128)S(1)} %get-tuple-element.7), channel_id=1, source_target_pairs={{0,1},{1,2},{2,3},{3,0},{4,5},{5,6},{6,7},{7,4},{8,9},{9,10},{10,1... | collective-permute-start | bytes 12488 | tf_op jit(solution)/shard_map/ppermute | solution.py:16
  20.6 3.8 %copy-start.1 = (f32[8,1,256]{1,0,2:T(8,128)S(1)}, f32[8,1,256]{1,0,2:T(8,128)}, u32[]{:S(2)}) copy-start(f32[8,1,256]{1,0,2:T(8,128)} %copy.62) | copy-start | bytes 24580
  20.6 3.8 %copy-start.2 = (f32[8,1,256]{1,0,2:T(8,128)S(1)}, f32[8,1,256]{1,0,2:T(8,128)}, u32[]{:S(2)}) copy-start(f32[8,1,256]{1,0,2:T(8,128)} %copy.64) | copy-start | bytes 24580
  20.6 3.8 %copy-start.4 = (bf16[8,128,256]{1,0,2:T(8,128)(2,1)S(1)}, bf16[8,128,256]{1,0,2:T(8,128)(2,1)}, u32[]{:S(2)}) copy-start(bf16[8,128,256]{1,0,2:T(8,128)(2,1)} %copy.72) | copy-start | bytes 1572868
  20.6 3.8 %copy-start.5 = (bf16[8,128,256]{1,0,2:T(8,128)(2,1)S(1)}, bf16[8,128,256]{1,0,2:T(8,128)(2,1)}, u32[]{:S(2)}) copy-start(bf16[8,128,256]{1,0,2:T(8,128)(2,1)} %copy.73) | copy-start | bytes 1572868
  20.6 3.8 %copy-start.6 = (bf16[8,128,256]{1,0,2:T(8,128)(2,1)S(1)}, bf16[8,128,256]{1,0,2:T(8,128)(2,1)}, u32[]{:S(2)}) copy-start(bf16[8,128,256]{1,0,2:T(8,128)(2,1)} %copy.74) | copy-start | bytes 1572868
  110.0 18.3 %copy-start.3 = (f32[8,128,256]{2,1,0:T(8,128)S(1)}, f32[8,128,256]{2,1,0:T(8,128)}, u32[]{:S(2)}) copy-start(f32[8,128,256]{2,1,0:T(8,128)} %param.6) | copy-start | bytes 3145732
where the time goes:
time: 130 us; the launch traced here: 129 us
  blocking collectives  77.5 us (60%)
  local copies, waits for them, and re-layouts  27 us (21%)
  other arithmetic  12.7 us (10%)
  starting transfers between devices  7.02 us (5%)
  matrix products  4.07 us (3%)
    all_to_all x1, blocking collectives, shards(): lax.all_to_all(section_two, 'py', split_axis=2, concat_axis=1, tiled=True)  28.2 us
    all_to_all x1, blocking collectives, shards(): lax.all_to_all(section_one, 'py', split_axis=1, concat_axis=2, tiled=True)  18.9 us
    all_to_all x1, blocking collectives, shards(): lax.all_to_all(lax.all_to_all(section_two, 'py', split_axis=2, concat_axi...  18.2 us
    unnamed x26, local copies, waits for them, and re-layouts  13 us
    all_to_all x1, blocking collectives, shards(): lax.all_to_all(rhs, 'px', split_axis=0, concat_axis=1, tiled=True)  12.2 us
    ppermute x2, starting transfers between devices, with_halo(): lax.ppermute(head, axis, [((i + 1) % count, i) for i in range(count)])  7.02 us
    unnamed x1, other arithmetic  4.59 us
    mul x1, other arithmetic, shards(): slope_y = jnp.pad(0.5 * (y_plus - y_minus), ((1, 1), (0, 0), (0, 0)))  3.77 us
  transfers between devices with their start and end apart: 4, of which 1 were waited for; matrix products, arithmetic and copies ran while one was open for 7% of the time, Pallas kernels for 0%

commit v1 on v0

--- a/solution.py
+++ b/solution.py
@@ -1,6 +1,10 @@
+import functools
+
 import jax
 import jax.numpy as jnp
 from jax import lax
+from jax.experimental import pallas as pl
+from jax.experimental.pallas import tpu as pltpu
 from jax.sharding import PartitionSpec as P
 
 time_step = 0.25
@@ -68,9 +72,328 @@
     return velocity + settled
 
 
+def send(src, dst, send_sem, recv_sem, target):
+    return pltpu.make_async_remote_copy(
+        src_ref=src,
+        dst_ref=dst,
+        send_sem=send_sem,
+        recv_sem=recv_sem,
+        device_id=target,
+        device_id_type=pl.DeviceIdType.MESH,
+    )
+
+
+def kernel(
+    npx,
+    npy,
+    vel_hbm,
+    frc_hbm,
+    cx_hbm,
+    cy_hbm,
+    ix_hbm,
+    iy_hbm,
+    out,
+    vel,
+    frc,
+    cx,
+    cy,
+    ix,
+    iy,
+    x_low,
+    x_high,
+    y_send,
+    y_recv,
+    slope_x,
+    slope_y,
+    lap,
+    rhs,
+    lines_x,
+    one,
+    lines_y,
+    two,
+    back,
+    load_sem,
+    halo_send,
+    halo_recv,
+    rhs_send,
+    rhs_recv,
+    one_send,
+    one_recv,
+    two_send,
+    two_recv,
+    out_send,
+    out_recv,
+    own_sem,
+):
+    me = lax.axis_index("px")
+    my = lax.axis_index("py")
+    levels, rows, cols = vel.shape
+    part = rows // npy
+    pieces = [(vel_hbm, vel), (frc_hbm, frc), (cx_hbm, cx), (cy_hbm, cy), (ix_hbm, ix), (iy_hbm, iy)]
+    loads = [pltpu.make_async_copy(a, b, load_sem.at[i]) for i, (a, b) in enumerate(pieces)]
+    for load in loads:
+        load.start()
+
+    barrier = pltpu.get_barrier_semaphore()
+    for step in range(1, npx):
+        pl.semaphore_signal(barrier, inc=1, device_id={"px": lax.rem(me + step, npx)}, device_id_type=pl.DeviceIdType.MESH)
+    for step in range(1, npy):
+        pl.semaphore_signal(barrier, inc=1, device_id={"py": lax.rem(my + step, npy)}, device_id_type=pl.DeviceIdType.MESH)
+
+    loads[0].wait()
+    lane = lax.broadcasted_iota(jnp.int32, (rows, 128), 1)
+
+    def gather_face(level, faces):
+        first, last = faces
+        now = vel[level]
+        first = jnp.where(lane == level, now[:, 0:1], first)
+        last = jnp.where(lane == level, now[:, cols - 1 : cols], last)
+        return first, last
+
+    zero = jnp.zeros((rows, 128), jnp.float32)
+    first, last = lax.fori_loop(0, levels, gather_face, (zero, zero))
+    y_send[0] = jnp.transpose(first)[:levels]
+    y_send[1] = jnp.transpose(last)[:levels]
+    pl.semaphore_wait(barrier, npx + npy - 2)
+
+    up_x, down_x = lax.rem(me + 1, npx), lax.rem(me + npx - 1, npx)
+    up_y, down_y = lax.rem(my + 1, npy), lax.rem(my + npy - 1, npy)
+    halos = [
+        send(y_send.at[1], y_recv.at[0], halo_send.at[0], halo_recv.at[0], {"py": up_y}),
+        send(y_send.at[0], y_recv.at[1], halo_send.at[1], halo_recv.at[1], {"py": down_y}),
+        send(vel.at[:, pl.ds(rows - 8, 8), :], x_low, halo_send.at[2], halo_recv.at[2], {"px": up_x}),
+        send(vel.at[:, pl.ds(0, 8), :], x_high, halo_send.at[3], halo_recv.at[3], {"px": down_x}),
+    ]
+    for halo in halos:
+        halo.start()
+    for halo in halos:
+        halo.wait_recv()
+
+    spare = jnp.zeros((128 - levels, rows), jnp.float32)
+    face_low = jnp.transpose(jnp.concatenate([y_recv[0], spare], axis=0))
+    face_high = jnp.transpose(jnp.concatenate([y_recv[1], spare], axis=0))
+    row_at = lax.broadcasted_iota(jnp.int32, (rows, cols), 0)
+    col_at = lax.broadcasted_iota(jnp.int32, (rows, cols), 1)
+    blank = jnp.zeros((rows, cols), jnp.float32)
+    for edge in (0, levels + 1):
+        slope_x[edge] = blank
+        slope_y[edge] = blank
+
+    def slopes(level, _):
+        now = vel[level]
+        low = jnp.sum(jnp.where(lane == level, face_low, 0.0), axis=1, keepdims=True)
+        high = jnp.sum(jnp.where(lane == level, face_high, 0.0), axis=1, keepdims=True)
+        x_minus = jnp.where(row_at == 0, x_low[level][7:8, :], pltpu.roll(now, 1, 0))
+        x_plus = jnp.where(row_at == rows - 1, x_high[level][0:1, :], pltpu.roll(now, rows - 1, 0))
+        y_minus = jnp.where(col_at == 0, low, pltpu.roll(now, 1, 1))
+        y_plus = jnp.where(col_at == cols - 1, high, pltpu.roll(now, cols - 1, 1))
+        slope_x[level + 1] = 0.5 * (x_plus - x_minus)
+        slope_y[level + 1] = 0.5 * (y_plus - y_minus)
+        lap[level] = x_plus + x_minus + y_plus + y_minus - 4.0 * now
+        return 0
+
+    lax.fori_loop(0, levels, slopes, 0)
+    for load in loads[1:4]:
+        load.wait()
+
+    def right_side(step, _):
+        level = lax.rem(me + 1 + step, npx)
+        above = jnp.minimum(level + 1, levels - 1)
+        below = jnp.maximum(level - 1, 0)
+        z_plus = jnp.where(level < levels - 1, 1.0, 0.0) * vel[above]
+        z_minus = jnp.where(level > 0, 1.0, 0.0) * vel[below]
+        total = lap[level] + z_plus + z_minus - 2.0 * vel[level]
+        total += cx[level].astype(jnp.float32) * (0.5 * (slope_x[level + 2] - slope_x[level]))
+        total += cy[level].astype(jnp.float32) * (0.5 * (slope_y[level + 2] - slope_y[level]))
+        total += frc[level].astype(jnp.float32)
+        value = (time_step * total).astype(jnp.bfloat16)
+
+        @pl.when(step < npx - 1)
+        def _():
+            rhs[level] = value
+            send(rhs.at[level], lines_x.at[me], rhs_send.at[level], rhs_recv.at[me], {"px": level}).start()
+
+        @pl.when(step == npx - 1)
+        def _():
+            lines_x[me] = value
+
+        return 0
+
+    lax.fori_loop(0, npx, right_side, 0)
+
+    def from_px(step):
+        other = lax.rem(me + step, npx)
+        return send(rhs.at[other], lines_x.at[other], rhs_send.at[other], rhs_recv.at[other], {"px": other})
+
+    loads[4].wait()
+
+    def wait_px(step, _):
+        from_px(step).wait_recv()
+        return 0
+
+    lax.fori_loop(1, npx, wait_px, 0)
+
+    def cut(at):
+        return pl.ds(pl.multiple_of(at * part, part), part)
+
+    def strip(at):
+        return pl.ds(pl.multiple_of(at * cols, cols), cols)
+
+    def to_y(step):
+        other = lax.rem(my + step, npy)
+        return send(one.at[other], lines_y.at[:, :, strip(my)], one_send.at[other], one_recv.at[my], {"py": other})
+
+    order_x = npx * rows
+    for step in [2, 1, 3, 0] if npy == 4 else [*range(1, npy), 0]:
+        other = lax.rem(my + step, npy)
+        mine = ix[:, cut(other), :].reshape(npx * part, order_x)
+        value = jnp.dot(mine, lines_x[...].reshape(order_x, cols), preferred_element_type=jnp.float32)
+        value = value.astype(jnp.bfloat16).reshape(npx, part, cols)
+        if step:
+            one[other] = value
+            to_y(step).start()
+        else:
+            lines_y[:, :, strip(my)] = value
+
+    loads[5].wait()
+    for step in range(1, npy):
+        other = lax.rem(my + step, npy)
+        send(one.at[other], lines_y.at[:, :, strip(other)], one_send.at[other], one_recv.at[other], {"py": other}).wait_recv()
+
+    def to_cells(step):
+        other = lax.rem(my + step, npy)
+        return send(two.at[other], back.at[my], two_send.at[other], two_recv.at[my], {"py": other})
+
+    order_y = npy * cols
+    for step in [2, 1, 3, 0] if npy == 4 else [*range(1, npy), 0]:
+        other = lax.rem(my + step, npy)
+        value = lax.dot_general(
+            lines_y[...].reshape(npx * part, order_y),
+            iy[strip(other), :],
+            (((1,), (1,)), ((), ())),
+            preferred_element_type=jnp.float32,
+        )
+        value = value.astype(jnp.bfloat16).reshape(npx, part, cols)
+        if step:
+            two[other] = value
+            to_cells(step).start()
+        else:
+            back[my] = value
+
+    def hand_on(origin, step):
+        other = lax.rem(me + step, npx)
+        return send(
+            back.at[origin, other], out.at[me, cut(origin), :], out_send.at[origin, other], out_recv.at[me], {"px": other}
+        )
+
+    def own(origin):
+        return pltpu.make_async_copy(back.at[origin, me], out.at[me, cut(origin), :], own_sem.at[origin])
+
+    for hop in [0, 1, 3, 2] if npy == 4 else range(npy):
+        origin = lax.rem(my + hop, npy)
+        if hop:
+            send(two.at[origin], back.at[origin], two_send.at[origin], two_recv.at[origin], {"py": origin}).wait_recv()
+
+        def give(step, _):
+            hand_on(origin, step).start()
+            return 0
+
+        lax.fori_loop(1, npx, give, 0)
+        own(origin).start()
+
+    def settle(step, _):
+        other = lax.rem(me + step, npx)
+        send(rhs.at[other], out.at[other], rhs_send.at[other], out_recv.at[other], {"px": other}).wait_recv()
+        from_px(step).wait_send()
+        return 0
+
+    lax.fori_loop(1, npx, settle, 0)
+    for halo in halos:
+        halo.wait_send()
+    for step in range(1, npy):
+        to_y(step).wait_send()
+        to_cells(step).wait_send()
+    for hop in range(npy):
+        origin = lax.rem(my + hop, npy)
+        own(origin).wait()
+
+        def sent(step, _):
+            hand_on(origin, step).wait_send()
+            return 0
+
+        lax.fori_loop(1, npx, sent, 0)
+
+
+def fused(velocity, forcing, cross_x, cross_y, inv_x, inv_y):
+    npx, npy = lax.axis_size("px"), lax.axis_size("py")
+    levels, rows, cols = velocity.shape
+    part = rows // npy
+    shape, narrow = velocity.shape, jnp.bfloat16
+    order_x, order_y = npx * rows, npy * cols
+    vmem, dma = pltpu.VMEM, pltpu.SemaphoreType.DMA
+    settled = pl.pallas_call(
+        functools.partial(kernel, npx, npy),
+        out_shape=jax.ShapeDtypeStruct(shape, narrow),
+        in_specs=[pl.BlockSpec(memory_space=pl.ANY)] * 6,
+        out_specs=pl.BlockSpec(memory_space=pl.ANY),
+        scratch_shapes=[
+            vmem(shape, jnp.float32),
+            vmem(shape, narrow),
+            vmem(shape, narrow),
+            vmem(shape, narrow),
+            vmem((npx, rows, order_x), narrow),
+            vmem((order_y, order_y), narrow),
+            vmem((levels, 8, cols), jnp.float32),
+            vmem((levels, 8, cols), jnp.float32),
+            vmem((2, levels, rows), jnp.float32),
+            vmem((2, levels, rows), jnp.float32),
+            vmem((levels + 2, rows, cols), jnp.float32),
+            vmem((levels + 2, rows, cols), jnp.float32),
+            vmem(shape, jnp.float32),
+            vmem(shape, narrow),
+            vmem((npx, rows, cols), narrow),
+            vmem((npy, npx, part, cols), narrow),
+            vmem((npx, part, order_y), narrow),
+            vmem((npy, npx, part, cols), narrow),
+            vmem((npy, npx, part, cols), narrow),
+            dma((6,)),
+            dma((4,)),
+            dma((4,)),
+            dma((npx,)),
+            dma((npx,)),
+            dma((npy,)),
+            dma((npy,)),
+            dma((npy,)),
+            dma((npy,)),
+            dma((npy, npx)),
+            dma((npx,)),
+            dma((npy,)),
+        ],
+        compiler_params=pltpu.CompilerParams(collective_id=0, has_side_effects=True, vmem_limit_bytes=48 * 1024 * 1024),
+        cost_estimate=pl.CostEstimate(flops=4 * order_x * order_y * rows, bytes_accessed=8 * 1024 * 1024, transcendentals=0),
+    )(
+        velocity,
+        forcing,
+        cross_x,
+        cross_y,
+        inv_x.reshape(npx, rows, order_x),
+        inv_y.reshape(order_y, order_y),
+    )
+    return velocity + settled.astype(jnp.float32)
+
+
+def step(velocity, forcing, cross_x, cross_y, inv_x, inv_y):
+    npx, npy = lax.axis_size("px"), lax.axis_size("py")
+    levels, rows, cols = velocity.shape
+    aligned = rows % (16 * npy) == 0 and rows % 128 == 0 and cols % 128 == 0 and levels % 8 == 0
+    if aligned and levels == npx and levels <= 128 and inv_x.shape[0] == 1:
+        return fused(velocity, forcing, cross_x, cross_y, inv_x, inv_y)
+    return shards(velocity, forcing, cross_x, cross_y, inv_x, inv_y)
+
+
 def solution(mesh):
     return jax.shard_map(
-        shards,
+        step,
         mesh=mesh,
         in_specs=(
             P(None, "px", "py"),

time: 130 us -> 57.3 us (0.44)
  blocking collectives: 77.5 us -> 0 us
  Pallas kernels: 0 us -> 49.8 us
  local copies, waits for them, and re-layouts: 27 us -> 5.94 us
  other arithmetic: 12.7 us -> 1.09 us
  starting transfers between devices: 7.02 us -> 0 us
  matrix products: 4.07 us -> 0 us
    all_to_all x4 -> x0, blocking collectives: 77.5 us -> none  [the longest x1 28.2 us: shards(): lax.all_to_all(section_two, 'py', split_axis=2, concat_axis=1, tiled=True)]
    pallas_call x0 -> x1, Pallas kernels: none -> 49.8 us  [fused(): pl.pallas_call(functools.partial(kernel, npx, npy), out_shape=jax.ShapeDt...]
    unnamed x26 -> x10, local copies, waits for them, and re-layouts: 13 us -> 5.94 us
    ppermute x4 -> x0, starting transfers between devices: 7.02 us -> none  [the longest x2 7.02 us: with_halo(): lax.ppermute(head, axis, [((i + 1) % count, i) for i in range(count)])]
    all_to_all x4 -> x0, local copies, waits for them, and re-layouts: 5.86 us -> none  [the longest x2 3.61 us: shards(): lax.all_to_all(section_two, 'py', split_axis=2, concat_axis=1, tiled=True)]
    unnamed x1 -> x0, other arithmetic: 4.59 us -> none
    dot_general x2 -> x0, matrix products: 4.07 us -> none  [the longest x1 2.52 us: shards(): jnp.einsum('lxb,lab->lxa', y_lines, inv_y, preferred_element_type=jnp.flo...]
    mul x1 -> x0, other arithmetic: 3.77 us -> none  [shards(): slope_y = jnp.pad(0.5 * (y_plus - y_minus), ((1, 1), (0, 0), (0, 0)))]
  transfers between devices with their start and end apart: 4 -> 0, of which waited for: 1 -> 0; matrix products, arithmetic and copies ran while one was open for 7% -> 0% of each run, Pallas kernels for 0% -> 0%
where the time goes in v1:
time: 57.3 us; the launch traced here: 56.9 us
  Pallas kernels  49.8 us (87%)
  local copies, waits for them, and re-layouts  5.94 us (10%)
  other arithmetic  1.09 us (2%)
    pallas_call x1, Pallas kernels, fused(): pl.pallas_call(functools.partial(kernel, npx, npy), out_shape=jax.ShapeDt...  49.8 us
    unnamed x10, local copies, waits for them, and re-layouts  5.94 us

profile of v1, /device:TPU:0, one launch (start us, length us, event | category | flops | bytes accessed | tf_op | source)
XLA Modules:
  0.0 56.9 jit_solution(8470745070962412636)
XLA Ops:
  0.0 0.0 copy-start
  0.0 1.2 %copy-done = f32[8,128,256]{2,1,0:T(8,128)S(1)} copy-done((f32[8,128,256]{2,1,0:T(8,128)S(1)}, f32[8,128,256]{2,1,0:T(8,128)}, u32[]{:S(2)}) %copy-start) | copy-done | bytes 1048600
  1.2 0.0 copy-start.1
  1.2 1.6 %copy-done.1 = bf16[1,1024,1024]{2,1,0:T(8,128)(2,1)S(1)} copy-done((bf16[1,1024,1024]{2,1,0:T(8,128)(2,1)S(1)}, bf16[1,1024,1024]{2,1,0:T(8,128)(2,1)}, u32[]{:S(2)}) %copy-start.1) | copy-done | bytes 2097176
  2.8 0.0 copy-start.2
  2.8 1.0 %copy-done.2 = bf16[8,128,256]{2,1,0:T(8,128)(2,1)S(1)} copy-done((bf16[8,128,256]{2,1,0:T(8,128)(2,1)S(1)}, bf16[8,128,256]{2,1,0:T(8,128)(2,1)}, u32[]{:S(2)}) %copy-start.2) | copy-done | bytes 524312
  3.9 0.0 copy-start.3
  3.9 1.0 %copy-done.3 = bf16[8,128,256]{2,1,0:T(8,128)(2,1)S(1)} copy-done((bf16[8,128,256]{2,1,0:T(8,128)(2,1)S(1)}, bf16[8,128,256]{2,1,0:T(8,128)(2,1)}, u32[]{:S(2)}) %copy-start.3) | copy-done | bytes 524312
  4.9 0.0 copy-start.4
  4.9 1.0 %copy-done.4 = bf16[8,128,256]{2,1,0:T(8,128)(2,1)S(1)} copy-done((bf16[8,128,256]{2,1,0:T(8,128)(2,1)S(1)}, bf16[8,128,256]{2,1,0:T(8,128)(2,1)}, u32[]{:S(2)}) %copy-start.4) | copy-done | bytes 524312
  5.9 49.8 %shard_map.64 = bf16[8,128,256]{2,1,0:T(8,128)(2,1)S(1)} custom-call(f32[8,128,256]{2,1,0:T(8,128)S(1)} %copy-done, bf16[8,128,256]{2,1,0:T(8,128)(2,1)S(1)} %copy-done.2, bf16[8,128,256]{2,1,0:T(8,128)(2,1)S(1)} %copy-done.3, bf16[8,128,256]{2,1,0:T(8,128)(2,1)S(1)} %copy-done.4, bf16[8,128,1024]{2,1,0:T(8,128)(2,1)S(1)} %bitcast.2, bf16[1024,1024]{1,0:T(8,128)(2,1)} %bitcast.3), custom_call_target="tpu_custom_call" | custom-call | flops 536870912 | bytes 8388608 | tf_op jit(solution)/shard_map/pallas_call | solution.py:334
  55.8 1.1 %convert_add_fusion = f32[8,128,256]{2,1,0:T(8,128)} fusion(f32[8,128,256]{2,1,0:T(8,128)S(1)} %copy-done, bf16[8,128,256]{2,1,0:T(8,128)(2,1)S(1)} %shard_map.64), kind=kLoop, calls=%fused_computation | loop fusion | flops 524288 | bytes 2621440 | tf_op jit(solution)/shard_map/add | solution.py:382
Async XLA Ops:
  0.0 1.2 %copy-start = (f32[8,128,256]{2,1,0:T(8,128)S(1)}, f32[8,128,256]{2,1,0:T(8,128)}, u32[]{:S(2)}) copy-start(f32[8,128,256]{2,1,0:T(8,128)} %vel_hbm.1) | copy-start | bytes 3145732
  1.2 1.6 %copy-start.1 = (bf16[1,1024,1024]{2,1,0:T(8,128)(2,1)S(1)}, bf16[1,1024,1024]{2,1,0:T(8,128)(2,1)}, u32[]{:S(2)}) copy-start(bf16[1,1024,1024]{2,1,0:T(8,128)(2,1)} %param.10) | copy-start | bytes 6291460
  2.8 1.0 %copy-start.2 = (bf16[8,128,256]{2,1,0:T(8,128)(2,1)S(1)}, bf16[8,128,256]{2,1,0:T(8,128)(2,1)}, u32[]{:S(2)}) copy-start(bf16[8,128,256]{2,1,0:T(8,128)(2,1)} %frc_hbm.1) | copy-start | bytes 1572868
  3.9 1.0 %copy-start.3 = (bf16[8,128,256]{2,1,0:T(8,128)(2,1)S(1)}, bf16[8,128,256]{2,1,0:T(8,128)(2,1)}, u32[]{:S(2)}) copy-start(bf16[8,128,256]{2,1,0:T(8,128)(2,1)} %cx_hbm.1) | copy-start | bytes 1572868
  4.9 1.0 %copy-start.4 = (bf16[8,128,256]{2,1,0:T(8,128)(2,1)S(1)}, bf16[8,128,256]{2,1,0:T(8,128)(2,1)}, u32[]{:S(2)}) copy-start(bf16[8,128,256]{2,1,0:T(8,128)(2,1)} %cy_hbm.1) | copy-start | bytes 1572868

commit v2 on v1

--- a/solution.py
+++ b/solution.py
@@ -129,6 +129,8 @@
     my = lax.axis_index("py")
     levels, rows, cols = vel.shape
     part = rows // npy
+    chunks = rhs.shape[0]
+    wide = cols // chunks
     pieces = [(vel_hbm, vel), (frc_hbm, frc), (cx_hbm, cx), (cy_hbm, cy), (ix_hbm, ix), (iy_hbm, iy)]
     loads = [pltpu.make_async_copy(a, b, load_sem.at[i]) for i, (a, b) in enumerate(pieces)]
     for load in loads:
@@ -196,138 +198,157 @@
     for load in loads[1:4]:
         load.wait()
 
-    def right_side(step, _):
-        level = lax.rem(me + 1 + step, npx)
+    def right_side(chunk, at):
+        level = lax.rem(me + 1 + at, npx)
+        side = slice(chunk * wide, (chunk + 1) * wide)
         above = jnp.minimum(level + 1, levels - 1)
         below = jnp.maximum(level - 1, 0)
-        z_plus = jnp.where(level < levels - 1, 1.0, 0.0) * vel[above]
-        z_minus = jnp.where(level > 0, 1.0, 0.0) * vel[below]
-        total = lap[level] + z_plus + z_minus - 2.0 * vel[level]
-        total += cx[level].astype(jnp.float32) * (0.5 * (slope_x[level + 2] - slope_x[level]))
-        total += cy[level].astype(jnp.float32) * (0.5 * (slope_y[level + 2] - slope_y[level]))
-        total += frc[level].astype(jnp.float32)
+        z_plus = jnp.where(level < levels - 1, 1.0, 0.0) * vel[above, :, side]
+        z_minus = jnp.where(level > 0, 1.0, 0.0) * vel[below, :, side]
+        total = lap[level, :, side] + z_plus + z_minus - 2.0 * vel[level, :, side]
+        total += cx[level, :, side].astype(jnp.float32) * (0.5 * (slope_x[level + 2, :, side] - slope_x[level, :, side]))
+        total += cy[level, :, side].astype(jnp.float32) * (0.5 * (slope_y[level + 2, :, side] - slope_y[level, :, side]))
+        total += frc[level, :, side].astype(jnp.float32)
         value = (time_step * total).astype(jnp.bfloat16)
 
-        @pl.when(step < npx - 1)
+        @pl.when(at < npx - 1)
         def _():
-            rhs[level] = value
-            send(rhs.at[level], lines_x.at[me], rhs_send.at[level], rhs_recv.at[me], {"px": level}).start()
-
-        @pl.when(step == npx - 1)
+            rhs[chunk, level] = value
+            to_px(chunk, level).start()
+
+        @pl.when(at == npx - 1)
         def _():
-            lines_x[me] = value
-
-        return 0
-
-    lax.fori_loop(0, npx, right_side, 0)
-
-    def from_px(step):
-        other = lax.rem(me + step, npx)
-        return send(rhs.at[other], lines_x.at[other], rhs_send.at[other], rhs_recv.at[other], {"px": other})
+            lines_x[chunk, me] = value
+
+    def to_px(chunk, other):
+        return send(
+            rhs.at[chunk, other], lines_x.at[chunk, me], rhs_send.at[chunk, other], rhs_recv.at[chunk, me], {"px": other}
+        )
+
+    def from_px(chunk, other):
+        return send(
+            rhs.at[chunk, other], lines_x.at[chunk, other], rhs_send.at[chunk, other], rhs_recv.at[chunk, other], {"px": other}
+        )
+
+    def over_px(body):
+        def one_step(at, _):
+            body(lax.rem(me + at, npx))
+            return 0
+
+        lax.fori_loop(1, npx, one_step, 0)
+
+    for chunk in range(chunks):
+        def one_level(at, _):
+            right_side(chunk, at)
+            return 0
+
+        lax.fori_loop(0, npx, one_level, 0)
+
+    half = part // 2
+    forward = [(chunk, 0, part) for chunk in range(chunks - 1)] + [(chunks - 1, 0, half), (chunks - 1, half, half)]
+    order = [2, 1, 3, 0] if npy == 4 else [*range(1, npy), 0]
+    order_x, order_y = npx * rows, npy * cols
+
+    def strip(at, chunk=0, width=cols):
+        return pl.ds(pl.multiple_of(at * cols + chunk * wide, wide), width)
+
+    def piece_y(index, other, source):
+        chunk, first, count = forward[index]
+        return send(
+            one.at[index, other, :, pl.ds(0, count)],
+            lines_y.at[:, pl.ds(first, count), strip(source, chunk, wide)],
+            one_send.at[index, other],
+            one_recv.at[index, source],
+            {"py": other},
+        )
 
     loads[4].wait()
-
-    def wait_px(step, _):
-        from_px(step).wait_recv()
-        return 0
-
-    lax.fori_loop(1, npx, wait_px, 0)
-
-    def cut(at):
-        return pl.ds(pl.multiple_of(at * part, part), part)
-
-    def strip(at):
-        return pl.ds(pl.multiple_of(at * cols, cols), cols)
-
-    def to_y(step):
-        other = lax.rem(my + step, npy)
-        return send(one.at[other], lines_y.at[:, :, strip(my)], one_send.at[other], one_recv.at[my], {"py": other})
-
-    order_x = npx * rows
-    for step in [2, 1, 3, 0] if npy == 4 else [*range(1, npy), 0]:
-        other = lax.rem(my + step, npy)
-        mine = ix[:, cut(other), :].reshape(npx * part, order_x)
-        value = jnp.dot(mine, lines_x[...].reshape(order_x, cols), preferred_element_type=jnp.float32)
-        value = value.astype(jnp.bfloat16).reshape(npx, part, cols)
-        if step:
-            one[other] = value
-            to_y(step).start()
-        else:
-            lines_y[:, :, strip(my)] = value
+    for index, (chunk, first, count) in enumerate(forward):
+        if first == 0:
+            over_px(lambda other: from_px(chunk, other).wait_recv())
+        for step in order:
+            other = lax.rem(my + step, npy)
+            mine = ix[:, pl.ds(pl.multiple_of(other * part + first, half), count), :].reshape(npx * count, order_x)
+            value = jnp.dot(mine, lines_x[chunk].reshape(order_x, wide), preferred_element_type=jnp.float32)
+            value = value.astype(jnp.bfloat16).reshape(npx, count, wide)
+            if step:
+                one[index, other, :, 0:count] = value
+                piece_y(index, other, my).start()
+            else:
+                lines_y[:, first : first + count, strip(my, chunk, wide)] = value
+
+    def piece_back(side, other, source):
+        return send(two.at[side, other], back.at[side, source], two_send.at[side, other], two_recv.at[side, source], {"py": other})
+
+    def cut(side, origin):
+        return pl.ds(pl.multiple_of(origin * part + side * half, half), half)
+
+    def hand_on(side, origin, other):
+        return send(
+            back.at[side, origin, other],
+            out.at[me, cut(side, origin), :],
+            out_send.at[side, origin, other],
+            out_recv.at[me],
+            {"px": other},
+        )
+
+    def own(side, origin):
+        return pltpu.make_async_copy(back.at[side, origin, me], out.at[me, cut(side, origin), :], own_sem.at[side, origin])
 
     loads[5].wait()
-    for step in range(1, npy):
-        other = lax.rem(my + step, npy)
-        send(one.at[other], lines_y.at[:, :, strip(other)], one_send.at[other], one_recv.at[other], {"py": other}).wait_recv()
-
-    def to_cells(step):
-        other = lax.rem(my + step, npy)
-        return send(two.at[other], back.at[my], two_send.at[other], two_recv.at[my], {"py": other})
-
-    order_y = npy * cols
-    for step in [2, 1, 3, 0] if npy == 4 else [*range(1, npy), 0]:
-        other = lax.rem(my + step, npy)
-        value = lax.dot_general(
-            lines_y[...].reshape(npx * part, order_y),
-            iy[strip(other), :],
-            (((1,), (1,)), ((), ())),
-            preferred_element_type=jnp.float32,
-        )
-        value = value.astype(jnp.bfloat16).reshape(npx, part, cols)
-        if step:
-            two[other] = value
-            to_cells(step).start()
-        else:
-            back[my] = value
-
-    def hand_on(origin, step):
-        other = lax.rem(me + step, npx)
-        return send(
-            back.at[origin, other], out.at[me, cut(origin), :], out_send.at[origin, other], out_recv.at[me], {"px": other}
-        )
-
-    def own(origin):
-        return pltpu.make_async_copy(back.at[origin, me], out.at[me, cut(origin), :], own_sem.at[origin])
-
-    for hop in [0, 1, 3, 2] if npy == 4 else range(npy):
-        origin = lax.rem(my + hop, npy)
-        if hop:
-            send(two.at[origin], back.at[origin], two_send.at[origin], two_recv.at[origin], {"py": origin}).wait_recv()
-
-        def give(step, _):
-            hand_on(origin, step).start()
-            return 0
-
-        lax.fori_loop(1, npx, give, 0)
-        own(origin).start()
-
-    def settle(step, _):
-        other = lax.rem(me + step, npx)
-        send(rhs.at[other], out.at[other], rhs_send.at[other], out_recv.at[other], {"px": other}).wait_recv()
-        from_px(step).wait_send()
-        return 0
-
-    lax.fori_loop(1, npx, settle, 0)
+    for side in range(2):
+        for index, (chunk, first, count) in enumerate(forward):
+            if first == side * half and (side == 1 or count > 0):
+                for step in range(1, npy):
+                    source = lax.rem(my + step, npy)
+                    piece_y(index, source, source).wait_recv()
+        held = lines_y[:, side * half : (side + 1) * half, :].reshape(npx * half, order_y)
+        for step in order:
+            other = lax.rem(my + step, npy)
+            value = lax.dot_general(held, iy[strip(other), :], (((1,), (1,)), ((), ())), preferred_element_type=jnp.float32)
+            value = value.astype(jnp.bfloat16).reshape(npx, half, cols)
+            if step:
+                two[side, other] = value
+                piece_back(side, other, my).start()
+            else:
+                back[side, my] = value
+
+    for side in range(2):
+        for hop in [0, 1, 3, 2] if npy == 4 else range(npy):
+            origin = lax.rem(my + hop, npy)
+            if hop:
+                piece_back(side, origin, origin).wait_recv()
+            over_px(lambda other: hand_on(side, origin, other).start())
+            own(side, origin).start()
+
+    def settle(other):
+        whole = send(out.at[other], out.at[other], rhs_send.at[0, other], out_recv.at[other], {"px": other})
+        whole.wait_recv()
+        for chunk in range(chunks):
+            to_px(chunk, other).wait_send()
+
+    over_px(settle)
     for halo in halos:
         halo.wait_send()
     for step in range(1, npy):
-        to_y(step).wait_send()
-        to_cells(step).wait_send()
-    for hop in range(npy):
-        origin = lax.rem(my + hop, npy)
-        own(origin).wait()
-
-        def sent(step, _):
-            hand_on(origin, step).wait_send()
-            return 0
-
-        lax.fori_loop(1, npx, sent, 0)
+        other = lax.rem(my + step, npy)
+        for index in range(len(forward)):
+            piece_y(index, other, my).wait_send()
+        for side in range(2):
+            piece_back(side, other, my).wait_send()
+    for side in range(2):
+        for hop in range(npy):
+            origin = lax.rem(my + hop, npy)
+            own(side, origin).wait()
+            over_px(lambda other: hand_on(side, origin, other).wait_send())
 
 
 def fused(velocity, forcing, cross_x, cross_y, inv_x, inv_y):
     npx, npy = lax.axis_size("px"), lax.axis_size("py")
     levels, rows, cols = velocity.shape
     part = rows // npy
+    half, chunks = part // 2, cols // 128
+    wide = cols // chunks
     shape, narrow = velocity.shape, jnp.bfloat16
     order_x, order_y = npx * rows, npy * cols
     vmem, dma = pltpu.VMEM, pltpu.SemaphoreType.DMA
@@ -350,26 +371,26 @@
             vmem((levels + 2, rows, cols), jnp.float32),
             vmem((levels + 2, rows, cols), jnp.float32),
             vmem(shape, jnp.float32),
-            vmem(shape, narrow),
-            vmem((npx, rows, cols), narrow),
-            vmem((npy, npx, part, cols), narrow),
+            vmem((chunks, levels, rows, wide), narrow),
+            vmem((chunks, npx, rows, wide), narrow),
+            vmem((chunks + 1, npy, npx, part, wide), narrow),
             vmem((npx, part, order_y), narrow),
-            vmem((npy, npx, part, cols), narrow),
-            vmem((npy, npx, part, cols), narrow),
+            vmem((2, npy, npx, half, cols), narrow),
+            vmem((2, npy, npx, half, cols), narrow),
             dma((6,)),
             dma((4,)),
             dma((4,)),
+            dma((chunks, npx)),
+            dma((chunks, npx)),
+            dma((chunks + 1, npy)),
+            dma((chunks + 1, npy)),
+            dma((2, npy)),
+            dma((2, npy)),
+            dma((2, npy, npx)),
             dma((npx,)),
-            dma((npx,)),
-            dma((npy,)),
-            dma((npy,)),
-            dma((npy,)),
-            dma((npy,)),
-            dma((npy, npx)),
-            dma((npx,)),
-            dma((npy,)),
+            dma((2, npy)),
         ],
-        compiler_params=pltpu.CompilerParams(collective_id=0, has_side_effects=True, vmem_limit_bytes=48 * 1024 * 1024),
+        compiler_params=pltpu.CompilerParams(collective_id=0, has_side_effects=True, vmem_limit_bytes=67_043_328),
         cost_estimate=pl.CostEstimate(flops=4 * order_x * order_y * rows, bytes_accessed=8 * 1024 * 1024, transcendentals=0),
     )(
         velocity,
@@ -385,7 +406,7 @@
 def step(velocity, forcing, cross_x, cross_y, inv_x, inv_y):
     npx, npy = lax.axis_size("px"), lax.axis_size("py")
     levels, rows, cols = velocity.shape
-    aligned = rows % (16 * npy) == 0 and rows % 128 == 0 and cols % 128 == 0 and levels % 8 == 0
+    aligned = rows % (32 * npy) == 0 and rows % 128 == 0 and cols % 128 == 0 and levels % 8 == 0
     if aligned and levels == npx and levels <= 128 and inv_x.shape[0] == 1:
         return fused(velocity, forcing, cross_x, cross_y, inv_x, inv_y)
     return shards(velocity, forcing, cross_x, cross_y, inv_x, inv_y)

time: 57.3 us -> 48.5 us (0.85)
  local copies, waits for them, and re-layouts: 5.94 us -> 0 us
  Pallas kernels: 49.8 us -> 45.4 us
  other arithmetic: 1.09 us -> 2.45 us
    unnamed x10 -> x0, local copies, waits for them, and re-layouts: 5.94 us -> none
    pallas_call x1, Pallas kernels: 49.8 us -> 45.4 us  [fused(): pl.pallas_call(functools.partial(kernel, npx, npy), out_shape=jax.ShapeDt...]
    add x1, other arithmetic: 1.09 us -> 2.45 us  [fused(): return velocity + settled.astype(jnp.float32)]
where the time goes in v2:
time: 48.5 us; the launch traced here: 47.8 us
  Pallas kernels  45.4 us (94%)
  other arithmetic  2.45 us (5%)
    pallas_call x1, Pallas kernels, fused(): pl.pallas_call(functools.partial(kernel, npx, npy), out_shape=jax.ShapeDt...  45.4 us
    add x1, other arithmetic, fused(): return velocity + settled.astype(jnp.float32)  2.45 us

profile of v2, /device:TPU:0, one launch (start us, length us, event | category | flops | bytes accessed | tf_op | source)
XLA Modules:
  0.0 47.8 jit_solution(13499268336605450417)
XLA Ops:
  0.0 45.4 %shard_map.64 = bf16[8,128,256]{2,1,0:T(8,128)(2,1)} custom-call(f32[8,128,256]{2,1,0:T(8,128)} %vel_hbm.1, bf16[8,128,256]{2,1,0:T(8,128)(2,1)} %frc_hbm.1, bf16[8,128,256]{2,1,0:T(8,128)(2,1)} %cx_hbm.1, bf16[8,128,256]{2,1,0:T(8,128)(2,1)} %cy_hbm.1, bf16[8,128,1024]{2,1,0:T(8,128)(2,1)} %bitcast.2, bf16[1024,1024]{1,0:T(8,128)(2,1)} %bitcast.3), custom_call_target="tpu_custom_call" | custom-call | flops 536870912 | bytes 8388608 | tf_op jit(solution)/shard_map/pallas_call | solution.py:355
  45.4 2.4 %convert_add_fusion = f32[8,128,256]{2,1,0:T(8,128)} fusion(f32[8,128,256]{2,1,0:T(8,128)} %vel_hbm.1, bf16[8,128,256]{2,1,0:T(8,128)(2,1)} %shard_map.64), kind=kLoop, calls=%fused_computation | loop fusion | flops 524288 | bytes 2621440 | tf_op jit(solution)/shard_map/add | solution.py:403

commit v3 on v2

--- a/solution.py
+++ b/solution.py
@@ -133,8 +133,7 @@
     wide = cols // chunks
     pieces = [(vel_hbm, vel), (frc_hbm, frc), (cx_hbm, cx), (cy_hbm, cy), (ix_hbm, ix), (iy_hbm, iy)]
     loads = [pltpu.make_async_copy(a, b, load_sem.at[i]) for i, (a, b) in enumerate(pieces)]
-    for load in loads:
-        load.start()
+    loads[0].start()
 
     barrier = pltpu.get_barrier_semaphore()
     for step in range(1, npx):
@@ -143,6 +142,8 @@
         pl.semaphore_signal(barrier, inc=1, device_id={"py": lax.rem(my + step, npy)}, device_id_type=pl.DeviceIdType.MESH)
 
     loads[0].wait()
+    for load in loads[1:]:
+        load.start()
     lane = lax.broadcasted_iota(jnp.int32, (rows, 128), 1)
 
     def gather_face(level, faces):
@@ -168,12 +169,6 @@
     ]
     for halo in halos:
         halo.start()
-    for halo in halos:
-        halo.wait_recv()
-
-    spare = jnp.zeros((128 - levels, rows), jnp.float32)
-    face_low = jnp.transpose(jnp.concatenate([y_recv[0], spare], axis=0))
-    face_high = jnp.transpose(jnp.concatenate([y_recv[1], spare], axis=0))
     row_at = lax.broadcasted_iota(jnp.int32, (rows, cols), 0)
     col_at = lax.broadcasted_iota(jnp.int32, (rows, cols), 1)
     blank = jnp.zeros((rows, cols), jnp.float32)
@@ -183,12 +178,10 @@
 
     def slopes(level, _):
         now = vel[level]
-        low = jnp.sum(jnp.where(lane == level, face_low, 0.0), axis=1, keepdims=True)
-        high = jnp.sum(jnp.where(lane == level, face_high, 0.0), axis=1, keepdims=True)
-        x_minus = jnp.where(row_at == 0, x_low[level][7:8, :], pltpu.roll(now, 1, 0))
-        x_plus = jnp.where(row_at == rows - 1, x_high[level][0:1, :], pltpu.roll(now, rows - 1, 0))
-        y_minus = jnp.where(col_at == 0, low, pltpu.roll(now, 1, 1))
-        y_plus = jnp.where(col_at == cols - 1, high, pltpu.roll(now, cols - 1, 1))
+        x_minus = jnp.where(row_at == 0, 0.0, pltpu.roll(now, 1, 0))
+        x_plus = jnp.where(row_at == rows - 1, 0.0, pltpu.roll(now, rows - 1, 0))
+        y_minus = jnp.where(col_at == 0, 0.0, pltpu.roll(now, 1, 1))
+        y_plus = jnp.where(col_at == cols - 1, 0.0, pltpu.roll(now, cols - 1, 1))
         slope_x[level + 1] = 0.5 * (x_plus - x_minus)
         slope_y[level + 1] = 0.5 * (y_plus - y_minus)
         lap[level] = x_plus + x_minus + y_plus + y_minus - 4.0 * now
@@ -198,17 +191,58 @@
     for load in loads[1:4]:
         load.wait()
 
+    def inner(level, _):
+        above = jnp.minimum(level + 1, levels - 1)
+        below = jnp.maximum(level - 1, 0)
+        z_plus = jnp.where(level < levels - 1, 1.0, 0.0) * vel[above]
+        z_minus = jnp.where(level > 0, 1.0, 0.0) * vel[below]
+        total = lap[level] + z_plus + z_minus - 2.0 * vel[level]
+        total += cx[level].astype(jnp.float32) * (0.5 * (slope_x[level + 2] - slope_x[level]))
+        total += cy[level].astype(jnp.float32) * (0.5 * (slope_y[level + 2] - slope_y[level]))
+        lap[level] = total + frc[level].astype(jnp.float32)
+        return 0
+
+    lax.fori_loop(0, levels, inner, 0)
+    for halo in halos:
+        halo.wait_recv()
+
+    def level_slope(face, axis, at):
+        size = face.shape[axis]
+        lower = jnp.where(at == 0, 0.0, pltpu.roll(face, 1, axis))
+        upper = jnp.where(at == levels - 1, 0.0, pltpu.roll(face, size - 1, axis))
+        return 0.25 * (upper - lower)
+
+    spare = jnp.zeros((128 - levels, rows), jnp.float32)
+    face_low = jnp.transpose(jnp.concatenate([y_recv[0], spare], axis=0))
+    face_high = jnp.transpose(jnp.concatenate([y_recv[1], spare], axis=0))
+    mixed_low = -level_slope(face_low, 1, lane)
+    mixed_high = level_slope(face_high, 1, lane)
+    level_at = lax.broadcasted_iota(jnp.int32, (levels, cols), 0)
+    x_face = (x_low[:, 7, :], x_high[:, 0, :])
+    x_mixed = (-level_slope(x_face[0], 0, level_at), level_slope(x_face[1], 0, level_at))
+    slab_at = lax.broadcasted_iota(jnp.int32, (16, wide), 0)
+    wide_at = lax.broadcasted_iota(jnp.int32, (rows, wide), 1)
+
     def right_side(chunk, at):
         level = lax.rem(me + 1 + at, npx)
         side = slice(chunk * wide, (chunk + 1) * wide)
-        above = jnp.minimum(level + 1, levels - 1)
-        below = jnp.maximum(level - 1, 0)
-        z_plus = jnp.where(level < levels - 1, 1.0, 0.0) * vel[above, :, side]
-        z_minus = jnp.where(level > 0, 1.0, 0.0) * vel[below, :, side]
-        total = lap[level, :, side] + z_plus + z_minus - 2.0 * vel[level, :, side]
-        total += cx[level, :, side].astype(jnp.float32) * (0.5 * (slope_x[level + 2, :, side] - slope_x[level, :, side]))
-        total += cy[level, :, side].astype(jnp.float32) * (0.5 * (slope_y[level + 2, :, side] - slope_y[level, :, side]))
-        total += frc[level, :, side].astype(jnp.float32)
+
+        def row(faces):
+            return jnp.sum(jnp.where(level_at[:, side] == level, faces, 0.0), axis=0, keepdims=True)
+
+        for end, first in enumerate((0, rows - 16)):
+            slab = slice(first, first + 16)
+            face = row(x_face[end][:, side]) + cx[level, slab, side].astype(jnp.float32) * row(x_mixed[end][:, side])
+            lap[level, slab, side] += jnp.where(slab_at == 15 * end, face, 0.0)
+        total = lap[level, :, side]
+
+        def column(faces):
+            return jnp.sum(jnp.where(lane == level, faces, 0.0), axis=1, keepdims=True)
+
+        for at_chunk, at_col, faces, mixed in ((0, 0, face_low, mixed_low), (chunks - 1, wide - 1, face_high, mixed_high)):
+            if chunk == at_chunk:
+                face = column(faces) + cy[level, :, side].astype(jnp.float32) * column(mixed)
+                total += jnp.where(wide_at == at_col, face, 0.0)
         value = (time_step * total).astype(jnp.bfloat16)
 
         @pl.when(at < npx - 1)
@@ -246,7 +280,12 @@
 
     half = part // 2
     forward = [(chunk, 0, part) for chunk in range(chunks - 1)] + [(chunks - 1, 0, half), (chunks - 1, half, half)]
-    order = [2, 1, 3, 0] if npy == 4 else [*range(1, npy), 0]
+    order = [*range(1, npy), 0]
+    turn = jnp.where(my < npy // 2, 1, npy - 1)
+
+    def mate(step):
+        return lax.rem(my + step * turn, npy)
+
     order_x, order_y = npx * rows, npy * cols
 
     def strip(at, chunk=0, width=cols):
@@ -267,7 +306,7 @@
         if first == 0:
             over_px(lambda other: from_px(chunk, other).wait_recv())
         for step in order:
-            other = lax.rem(my + step, npy)
+            other = mate(step)
             mine = ix[:, pl.ds(pl.multiple_of(other * part + first, half), count), :].reshape(npx * count, order_x)
             value = jnp.dot(mine, lines_x[chunk].reshape(order_x, wide), preferred_element_type=jnp.float32)
             value = value.astype(jnp.bfloat16).reshape(npx, count, wide)
@@ -304,7 +343,7 @@
                     piece_y(index, source, source).wait_recv()
         held = lines_y[:, side * half : (side + 1) * half, :].reshape(npx * half, order_y)
         for step in order:
-            other = lax.rem(my + step, npy)
+            other = mate(step)
             value = lax.dot_general(held, iy[strip(other), :], (((1,), (1,)), ((), ())), preferred_element_type=jnp.float32)
             value = value.astype(jnp.bfloat16).reshape(npx, half, cols)
             if step:

time: 48.5 us -> 48 us (0.990)
  no operation moved by 1% of the time
where the time goes in v3:
time: 48 us; the launch traced here: 47.8 us
  Pallas kernels  45.4 us (95%)
  other arithmetic  2.45 us (5%)
    pallas_call x1, Pallas kernels, fused(): pl.pallas_call(functools.partial(kernel, npx, npy), out_shape=jax.ShapeDt...  45.4 us
    add x1, other arithmetic, fused(): return velocity + settled.astype(jnp.float32)  2.45 us

profile of v3, /device:TPU:0, one launch (start us, length us, event | category | flops | bytes accessed | tf_op | source)
XLA Modules:
  0.0 47.8 jit_solution(16507255031376577547)
XLA Ops:
  0.0 45.4 %shard_map.64 = bf16[8,128,256]{2,1,0:T(8,128)(2,1)} custom-call(f32[8,128,256]{2,1,0:T(8,128)} %vel_hbm.1, bf16[8,128,256]{2,1,0:T(8,128)(2,1)} %frc_hbm.1, bf16[8,128,256]{2,1,0:T(8,128)(2,1)} %cx_hbm.1, bf16[8,128,256]{2,1,0:T(8,128)(2,1)} %cy_hbm.1, bf16[8,128,1024]{2,1,0:T(8,128)(2,1)} %bitcast.2, bf16[1024,1024]{1,0:T(8,128)(2,1)} %bitcast.3), custom_call_target="tpu_custom_call" | custom-call | flops 536870912 | bytes 8388608 | tf_op jit(solution)/shard_map/pallas_call | solution.py:394
  45.4 2.4 %convert_add_fusion = f32[8,128,256]{2,1,0:T(8,128)} fusion(f32[8,128,256]{2,1,0:T(8,128)} %vel_hbm.1, bf16[8,128,256]{2,1,0:T(8,128)(2,1)} %shard_map.64), kind=kLoop, calls=%fused_computation | loop fusion | flops 524288 | bytes 2621440 | tf_op jit(solution)/shard_map/add | solution.py:442

commit v4 on v3

--- a/solution.py
+++ b/solution.py
@@ -111,7 +111,6 @@
     one,
     lines_y,
     two,
-    back,
     load_sem,
     halo_send,
     halo_recv,
@@ -120,10 +119,7 @@
     one_send,
     one_recv,
     two_send,
-    two_recv,
-    out_send,
     out_recv,
-    own_sem,
 ):
     me = lax.axis_index("px")
     my = lax.axis_index("py")
@@ -316,28 +312,25 @@
             else:
                 lines_y[:, first : first + count, strip(my, chunk, wide)] = value
 
-    def piece_back(side, other, source):
-        return send(two.at[side, other], back.at[side, source], two_send.at[side, other], two_recv.at[side, source], {"py": other})
-
     def cut(side, origin):
         return pl.ds(pl.multiple_of(origin * part + side * half, half), half)
 
-    def hand_on(side, origin, other):
+    def to_cells(side, other_y, other_x):
         return send(
-            back.at[side, origin, other],
-            out.at[me, cut(side, origin), :],
-            out_send.at[side, origin, other],
+            two.at[side, other_y, other_x],
+            out.at[me, cut(side, my), :],
+            two_send.at[side, other_y, other_x],
             out_recv.at[me],
-            {"px": other},
+            {"px": other_x, "py": other_y},
         )
 
-    def own(side, origin):
-        return pltpu.make_async_copy(back.at[side, origin, me], out.at[me, cut(side, origin), :], own_sem.at[side, origin])
+    def own(side):
+        return pltpu.make_async_copy(two.at[side, my, me], out.at[me, cut(side, my), :], out_recv.at[me])
 
     loads[5].wait()
     for side in range(2):
         for index, (chunk, first, count) in enumerate(forward):
-            if first == side * half and (side == 1 or count > 0):
+            if first == side * half:
                 for step in range(1, npy):
                     source = lax.rem(my + step, npy)
                     piece_y(index, source, source).wait_recv()
@@ -345,41 +338,32 @@
         for step in order:
             other = mate(step)
             value = lax.dot_general(held, iy[strip(other), :], (((1,), (1,)), ((), ())), preferred_element_type=jnp.float32)
-            value = value.astype(jnp.bfloat16).reshape(npx, half, cols)
+            two[side, other] = value.astype(jnp.bfloat16).reshape(npx, half, cols)
+            over_px(lambda other_x: to_cells(side, other, other_x).start())
             if step:
-                two[side, other] = value
-                piece_back(side, other, my).start()
+                to_cells(side, other, me).start()
             else:
-                back[side, my] = value
-
-    for side in range(2):
-        for hop in [0, 1, 3, 2] if npy == 4 else range(npy):
-            origin = lax.rem(my + hop, npy)
-            if hop:
-                piece_back(side, origin, origin).wait_recv()
-            over_px(lambda other: hand_on(side, origin, other).start())
-            own(side, origin).start()
+                own(side).start()
 
     def settle(other):
-        whole = send(out.at[other], out.at[other], rhs_send.at[0, other], out_recv.at[other], {"px": other})
-        whole.wait_recv()
+        send(out.at[other], out.at[other], rhs_send.at[0, other], out_recv.at[other], {"px": other}).wait_recv()
         for chunk in range(chunks):
             to_px(chunk, other).wait_send()
 
     over_px(settle)
+    pltpu.make_async_copy(out.at[me], out.at[me], out_recv.at[me]).wait()
     for halo in halos:
         halo.wait_send()
     for step in range(1, npy):
         other = lax.rem(my + step, npy)
         for index in range(len(forward)):
             piece_y(index, other, my).wait_send()
-        for side in range(2):
-            piece_back(side, other, my).wait_send()
     for side in range(2):
-        for hop in range(npy):
-            origin = lax.rem(my + hop, npy)
-            own(side, origin).wait()
-            over_px(lambda other: hand_on(side, origin, other).wait_send())
+        for step in range(npy):
+            other = lax.rem(my + step, npy)
+            over_px(lambda other_x: to_cells(side, other, other_x).wait_send())
+            if step:
+                to_cells(side, other, me).wait_send()
 
 
 def fused(velocity, forcing, cross_x, cross_y, inv_x, inv_y):
@@ -415,7 +399,6 @@
             vmem((chunks + 1, npy, npx, part, wide), narrow),
             vmem((npx, part, order_y), narrow),
             vmem((2, npy, npx, half, cols), narrow),
-            vmem((2, npy, npx, half, cols), narrow),
             dma((6,)),
             dma((4,)),
             dma((4,)),
@@ -423,11 +406,8 @@
             dma((chunks, npx)),
             dma((chunks + 1, npy)),
             dma((chunks + 1, npy)),
-            dma((2, npy)),
-            dma((2, npy)),
             dma((2, npy, npx)),
             dma((npx,)),
-            dma((2, npy)),
         ],
         compiler_params=pltpu.CompilerParams(collective_id=0, has_side_effects=True, vmem_limit_bytes=67_043_328),
         cost_estimate=pl.CostEstimate(flops=4 * order_x * order_y * rows, bytes_accessed=8 * 1024 * 1024, transcendentals=0),

time: 48 us -> 44.8 us (0.933)
  Pallas kernels: 45.4 us -> 42.2 us
    pallas_call x1, Pallas kernels: 45.4 us -> 42.2 us  [fused(): pl.pallas_call(functools.partial(kernel, npx, npy), out_shape=jax.ShapeDt...]
where the time goes in v4:
time: 44.8 us; the launch traced here: 44.6 us
  Pallas kernels  42.2 us (94%)
  other arithmetic  2.45 us (5%)
    pallas_call x1, Pallas kernels, fused(): pl.pallas_call(functools.partial(kernel, npx, npy), out_shape=jax.ShapeDt...  42.2 us
    add x1, other arithmetic, fused(): return velocity + settled.astype(jnp.float32)  2.45 us

profile of v4, /device:TPU:0, one launch (start us, length us, event | category | flops | bytes accessed | tf_op | source)
XLA Modules:
  0.0 44.6 jit_solution(8150112597946751314)
XLA Ops:
  0.0 42.2 %shard_map.64 = bf16[8,128,256]{2,1,0:T(8,128)(2,1)} custom-call(f32[8,128,256]{2,1,0:T(8,128)} %vel_hbm.1, bf16[8,128,256]{2,1,0:T(8,128)(2,1)} %frc_hbm.1, bf16[8,128,256]{2,1,0:T(8,128)(2,1)} %cx_hbm.1, bf16[8,128,256]{2,1,0:T(8,128)(2,1)} %cy_hbm.1, bf16[8,128,1024]{2,1,0:T(8,128)(2,1)} %bitcast.2, bf16[1024,1024]{1,0:T(8,128)(2,1)} %bitcast.3), custom_call_target="tpu_custom_call" | custom-call | flops 536870912 | bytes 8388608 | tf_op jit(solution)/shard_map/pallas_call | solution.py:378
  42.2 2.4 %convert_add_fusion = f32[8,128,256]{2,1,0:T(8,128)} fusion(f32[8,128,256]{2,1,0:T(8,128)} %vel_hbm.1, bf16[8,128,256]{2,1,0:T(8,128)(2,1)} %shard_map.64), kind=kLoop, calls=%fused_computation | loop fusion | flops 524288 | bytes 2621440 | tf_op jit(solution)/shard_map/add | solution.py:422

commit v5 on v4

--- a/solution.py
+++ b/solution.py
@@ -409,7 +409,7 @@
             dma((2, npy, npx)),
             dma((npx,)),
         ],
-        compiler_params=pltpu.CompilerParams(collective_id=0, has_side_effects=True, vmem_limit_bytes=67_043_328),
+        compiler_params=pltpu.CompilerParams(collective_id=0, has_side_effects=True, vmem_limit_bytes=56_000_000),
         cost_estimate=pl.CostEstimate(flops=4 * order_x * order_y * rows, bytes_accessed=8 * 1024 * 1024, transcendentals=0),
     )(
         velocity,

time: 44.8 us -> 43.4 us (0.969)
  other arithmetic: 2.45 us -> 1.09 us
    add x1, other arithmetic: 2.45 us -> 1.09 us  [fused(): return velocity + settled.astype(jnp.float32)]
where the time goes in v5:
time: 43.4 us; the launch traced here: 43.3 us
  Pallas kernels  42.2 us (97%)
  other arithmetic  1.09 us (3%)
    pallas_call x1, Pallas kernels, fused(): pl.pallas_call(functools.partial(kernel, npx, npy), out_shape=jax.ShapeDt...  42.2 us
    add x1, other arithmetic, fused(): return velocity + settled.astype(jnp.float32)  1.09 us

profile of v5, /device:TPU:0, one launch (start us, length us, event | category | flops | bytes accessed | tf_op | source)
XLA Modules:
  0.0 43.3 jit_solution(16214635934914355547)
XLA Ops:
  0.0 0.0 copy-start
  0.0 42.2 %shard_map.64 = bf16[8,128,256]{2,1,0:T(8,128)(2,1)S(1)} custom-call(f32[8,128,256]{2,1,0:T(8,128)} %vel_hbm.1, bf16[8,128,256]{2,1,0:T(8,128)(2,1)} %frc_hbm.1, bf16[8,128,256]{2,1,0:T(8,128)(2,1)} %cx_hbm.1, bf16[8,128,256]{2,1,0:T(8,128)(2,1)} %cy_hbm.1, bf16[8,128,1024]{2,1,0:T(8,128)(2,1)} %bitcast.2, bf16[1024,1024]{1,0:T(8,128)(2,1)} %bitcast.3), custom_call_target="tpu_custom_call" | custom-call | flops 536870912 | bytes 8388608 | tf_op jit(solution)/shard_map/pallas_call | solution.py:378
  42.2 0.0 copy-done
  42.2 1.1 %convert_add_fusion = f32[8,128,256]{2,1,0:T(8,128)} fusion(f32[8,128,256]{2,1,0:T(8,128)S(1)} %copy-done, bf16[8,128,256]{2,1,0:T(8,128)(2,1)S(1)} %shard_map.64), kind=kLoop, calls=%fused_computation | loop fusion | flops 524288 | bytes 2621440 | tf_op jit(solution)/shard_map/add | solution.py:422
Async XLA Ops:
  0.0 42.2 %copy-start = (f32[8,128,256]{2,1,0:T(8,128)S(1)}, f32[8,128,256]{2,1,0:T(8,128)}, u32[]{:S(2)}) copy-start(f32[8,128,256]{2,1,0:T(8,128)} %vel_hbm.1) | copy-start | bytes 3145732

commit v6 on v5

--- a/solution.py
+++ b/solution.py
@@ -220,7 +220,8 @@
     wide_at = lax.broadcasted_iota(jnp.int32, (rows, wide), 1)
 
     def right_side(chunk, at):
-        level = lax.rem(me + 1 + at, npx)
+        ahead = jnp.where(at == npx - 1, 0, lax.rem(at + npx // 4, npx - 1) + 1)
+        level = lax.rem(me + ahead, npx)
         side = slice(chunk * wide, (chunk + 1) * wide)
 
         def row(faces):

time: 43.4 us -> 43.6 us (level)
  no operation moved by 1% of the time
where the time goes in v6:
time: 43.6 us; the launch traced here: 43.5 us
  Pallas kernels  42.4 us (97%)
  other arithmetic  1.09 us (3%)
    pallas_call x1, Pallas kernels, fused(): pl.pallas_call(functools.partial(kernel, npx, npy), out_shape=jax.ShapeDt...  42.4 us
    add x1, other arithmetic, fused(): return velocity + settled.astype(jnp.float32)  1.09 us

profile of v6, /device:TPU:0, one launch (start us, length us, event | category | flops | bytes accessed | tf_op | source)
XLA Modules:
  0.0 43.5 jit_solution(10584554902411692528)
XLA Ops:
  0.0 0.0 copy-start
  0.0 42.4 %shard_map.64 = bf16[8,128,256]{2,1,0:T(8,128)(2,1)S(1)} custom-call(f32[8,128,256]{2,1,0:T(8,128)} %vel_hbm.1, bf16[8,128,256]{2,1,0:T(8,128)(2,1)} %frc_hbm.1, bf16[8,128,256]{2,1,0:T(8,128)(2,1)} %cx_hbm.1, bf16[8,128,256]{2,1,0:T(8,128)(2,1)} %cy_hbm.1, bf16[8,128,1024]{2,1,0:T(8,128)(2,1)} %bitcast.2, bf16[1024,1024]{1,0:T(8,128)(2,1)} %bitcast.3), custom_call_target="tpu_custom_call" | custom-call | flops 536870912 | bytes 8388608 | tf_op jit(solution)/shard_map/pallas_call | solution.py:379
  42.4 0.0 copy-done
  42.4 1.1 %convert_add_fusion = f32[8,128,256]{2,1,0:T(8,128)} fusion(f32[8,128,256]{2,1,0:T(8,128)S(1)} %copy-done, bf16[8,128,256]{2,1,0:T(8,128)(2,1)S(1)} %shard_map.64), kind=kLoop, calls=%fused_computation | loop fusion | flops 524288 | bytes 2621440 | tf_op jit(solution)/shard_map/add | solution.py:423
Async XLA Ops:
  0.0 42.4 %copy-start = (f32[8,128,256]{2,1,0:T(8,128)S(1)}, f32[8,128,256]{2,1,0:T(8,128)}, u32[]{:S(2)}) copy-start(f32[8,128,256]{2,1,0:T(8,128)} %vel_hbm.1) | copy-start | bytes 3145732
